TPU v7x, 32 devices: a whole 2x2x4 slice. The times are simulated.
32 devices in a mesh: dp: 8 (over y, x, core), mp: 4 (over z).
Axes of the slice: x: 2, y: 2, z: 4, core: 2. Of those that a mesh axis runs over, the one named last changes fastest.
Arguments:
- tokens: bfloat16 [32768, 512], P(('dp', 'mp')), may hold values from -6 to 6
- qkv_weight: bfloat16 [512, 1536], replicated, may hold values from -0.25 to 0.25
- out_weight: bfloat16 [512, 512], replicated, may hold values from -2 to 2
- norm1_gain: float32 [512], replicated, may hold values from 0.1 to 1.9
- norm1_shift: float32 [512], replicated, may hold values from -3 to 3
- norm2_gain: float32 [512], replicated, may hold values from 0.1 to 1.9
- norm2_shift: float32 [512], replicated, may hold values from -3 to 3
- up_weight: bfloat16 [512, 2048], P(None, 'mp'), may hold values from -0.25 to 0.25
- up_bias: bfloat16 [2048], P('mp'), may hold values from -3 to 3
- down_weight: bfloat16 [2048, 512], P('mp'), may hold values from -0.125 to 0.125
- down_bias: float32 [512], replicated, may hold values from -3 to 3
- lengths: int32 [17], replicated, may hold values from 512 to 16384, as said below
- cotangent: bfloat16 [32768, 512], P(('dp', 'mp')), may hold values from -6 to 6
Outputs:
- output: bfloat16 [32768, 512], P(('dp', 'mp'))
- input_grad: bfloat16 [32768, 512], P(('dp', 'mp'))
- qkv_grad: float32 [512, 1536], replicated
- out_grad: float32 [512, 512], replicated
- norm1_gain_grad: float32 [512], replicated
- norm1_shift_grad: float32 [512], replicated
- norm2_gain_grad: float32 [512], replicated
- norm2_shift_grad: float32 [512], replicated
- up_grad: float32 [512, 2048], P(None, 'mp')
- up_bias_grad: float32 [2048], P('mp')
- down_grad: float32 [2048, 512], P('mp')
- down_bias_grad: float32 [512], replicated
Inputs may be any that keep to these rules, and one draw needn't show every extreme that they name: The 17 lengths add up to 32768; 1 of them equal 16384, and the others lie between 512 and 1536, both ends reached.
All inputs are finite; a program needn't handle non-finite values.
Results may differ from a plain program's by a relative error of at most 0.012.
Values may be sent and summed in bfloat16 or wider, within the bound.
No kernel may reach another device: no remote copies, remote signals or barrier semaphores. Data moves between devices by JAX's collectives and lax.ppermute only.
A program may use at most 192 MiB of HBM per device.

v0:
```python
import jax
import jax.numpy as jnp
from jax import lax
from jax.sharding import PartitionSpec as P

HEADS = 8
HEAD_DIM = 64
BLK = 512
NORM_EPS = 1e-05
SCORE_EPS = 1e-06
EXACT_MODE = lax.Precision.HIGHEST


def carried_in(array, axis, combine, identity):
    peers, position = (lax.axis_size(axis), lax.axis_index(axis))
    everything = jax.tree.map(
        lambda part, kind: lax.all_gather(part.astype(kind), axis),
        array,
        (jnp.bfloat16, jnp.bfloat16, jnp.bfloat16),
    )
    start = jax.tree.map(
        lambda part, zero: jnp.broadcast_to(jnp.asarray(zero, part.dtype), part.shape),
        array,
        identity,
    )

    def lap(k, before):
        reached = k < position
        new = combine(
            before, jax.tree.map(lambda part, own: part[k].astype(own.dtype), everything, array)
        )
        return jax.tree.map(lambda a, b: jnp.where(reached, a, b), new, before)

    return lax.fori_loop(0, peers, lap, start)


def carried_in_2(array, axis, join, neutral):
    count = lax.axis_size(axis)
    place = lax.axis_index(axis)
    ahead = count - 1 - place
    gathered = jax.tree.map(
        lambda a, kind: lax.all_gather(a.astype(kind), axis),
        array,
        jax.tree.map(lambda a: jnp.bfloat16 if a.dtype == jnp.float32 else a.dtype, array),
    )
    state = jax.tree.map(lambda a, e: jnp.zeros_like(a) + jnp.asarray(e, a.dtype), array, neutral)

    def one(lap, state):
        source = count - 1 - lap
        return join(
            state,
            jax.tree.map(
                lambda a, own: lax.dynamic_index_in_dim(a, source, 0, False).astype(own.dtype),
                gathered,
                array,
            ),
        )

    return lax.fori_loop(0, ahead, one, state)


def normalize(rows, gain, shift):
    centred = rows - jnp.mean(rows, axis=-1, keepdims=True)
    inv_std = lax.rsqrt(jnp.mean(centred * centred, axis=-1, keepdims=True) + NORM_EPS)
    scaled = centred * inv_std
    return (scaled * gain + shift, scaled, inv_std)


def normalize_back(upstream, scaled, inv_std, gain):
    weighted = upstream * gain
    centred = weighted - jnp.mean(weighted, axis=-1, keepdims=True)
    inner = centred - scaled * jnp.mean(weighted * scaled, axis=-1, keepdims=True)
    return (inner * inv_std, jnp.sum(upstream * scaled, axis=0), jnp.sum(upstream, axis=0))


def feature_map(values):
    return jax.nn.elu(values) + 1.0


def feature_slope(values):
    return jnp.where(values > 0, 1.0, jnp.exp(jnp.minimum(values, 0.0)))


def gelu_slope(values):
    return (
        0.5 * (1.0 + lax.erf(values * 0.7071067811865476))
        + values * jnp.exp(-0.5 * values * values) * 0.3989422804014327
    )


def segment_rows(lengths, first, count):
    ends = jnp.cumsum(lengths)
    starts = ends - lengths
    places = first + jnp.arange(count, dtype=jnp.int32)
    segment = jnp.sum((ends[None, :] <= places[:, None]).astype(jnp.int32), axis=1)
    opening = jnp.sum((starts[None, :] == places[:, None]).astype(jnp.int32), axis=1)
    return (segment, opening)


def block_masks(segment, opening, start):
    block_seg = lax.dynamic_slice_in_dim(segment, start, BLK)
    first_open = lax.dynamic_slice_in_dim(opening, start, 1)[0]
    carried = ((block_seg == block_seg[0]) & (first_open == 0)).astype(jnp.float32)
    ending = (block_seg == block_seg[-1]).astype(jnp.float32)
    places = jnp.arange(BLK)
    allowed = (
        (places[None, :] <= places[:, None]) & (block_seg[None, :] == block_seg[:, None])
    ).astype(jnp.float32)
    return (carried, ending, allowed)


def join_states(earlier, later):
    keep = 1.0 - later[2]
    return (
        later[0] + keep * earlier[0],
        later[1] + keep * earlier[1],
        jnp.maximum(earlier[2], later[2]),
    )


def local(
    tokens,
    qkv_weight,
    out_weight,
    norm1_gain,
    norm1_shift,
    norm2_gain,
    norm2_shift,
    up_weight,
    up_bias,
    down_weight,
    down_bias,
    lengths,
    cotangent,
):
    rows = tokens.shape[0]
    width = tokens.shape[1]
    span = rows * lax.axis_size("mp")
    blocks = span // BLK
    group_first = lax.axis_index("dp") * span
    own_start = lax.axis_index("mp") * rows
    segment, opening = segment_rows(lengths, group_first, span)
    continuing = ((segment == segment[0]) & (opening[0] == 0)).astype(jnp.float32)
    reset = 1.0 - continuing[-1]
    inputs = tokens.astype(jnp.float32)
    normed_one, scaled_one, inv_one = normalize(inputs, norm1_gain, norm1_shift)
    normed_low = normed_one.astype(jnp.bfloat16)
    group_rows = lax.all_gather(normed_low, "mp", axis=0, tiled=True)

    def features(start):
        rows_in = lax.dynamic_slice_in_dim(group_rows, start, BLK)
        projected = jnp.dot(rows_in, qkv_weight, preferred_element_type=jnp.float32)
        query = projected[:, :width].reshape(BLK, HEADS, HEAD_DIM)
        keys = projected[:, width : 2 * width].reshape(BLK, HEADS, HEAD_DIM)
        values = projected[:, 2 * width :].reshape(BLK, HEADS, HEAD_DIM)
        return (query, keys, values)

    def forward_block(carry, index):
        state, total = carry
        start = index * BLK
        query, keys, values = features(start)
        query_low = feature_map(query).astype(jnp.bfloat16)
        key_low = feature_map(keys).astype(jnp.bfloat16)
        value_low = values.astype(jnp.bfloat16)
        carried, ending, allowed = block_masks(segment, opening, start)
        scores = (
            jnp.einsum("ihd,jhd->hij", query_low, key_low, preferred_element_type=jnp.float32)
            * allowed[None]
        )
        query_wide = query_low.astype(jnp.float32)
        numerator = jnp.einsum(
            "hij,jhd->ihd",
            scores.astype(jnp.bfloat16),
            value_low,
            preferred_element_type=jnp.float32,
        )
        numerator = numerator + carried[:, None, None] * jnp.einsum(
            "ihd,hde->ihe", query_wide, state, precision=EXACT_MODE
        )
        denominator = (
            jnp.sum(scores, axis=-1).T
            + carried[:, None] * jnp.einsum("ihd,hd->ih", query_wide, total, precision=EXACT_MODE)
            + SCORE_EPS
        )
        keep = carried[-1]
        key_end = key_low * ending.astype(jnp.bfloat16)[:, None, None]
        new_state = keep * state + jnp.einsum(
            "jhd,jhe->hde", key_end, value_low, preferred_element_type=jnp.float32
        )
        new_total = keep * total + jnp.sum(key_end.astype(jnp.float32), axis=0)
        return ((new_state, new_total), (numerator, denominator, query_low, state, total))

    zero_state = jnp.zeros((HEADS, HEAD_DIM, HEAD_DIM), jnp.float32)
    zero_total = jnp.zeros((HEADS, HEAD_DIM), jnp.float32)
    nothing = jnp.zeros((), jnp.float32)
    (state_end, total_end), kept = lax.scan(
        forward_block, (zero_state, zero_total), jnp.arange(blocks, dtype=jnp.int32)
    )
    numerator = kept[0].reshape(span, HEADS, HEAD_DIM)
    denominator = kept[1].reshape(span, HEADS)
    query_all = kept[2].reshape(span, HEADS, HEAD_DIM)
    block_states = kept[3]
    block_totals = kept[4]
    state_in, total_in, _ = carried_in(
        (state_end, total_end, reset), "dp", join_states, (zero_state, zero_total, nothing)
    )
    query_wide = query_all.astype(jnp.float32)
    numerator = numerator + continuing[:, None, None] * jnp.einsum(
        "ihd,hde->ihe", query_wide, state_in, precision=EXACT_MODE
    )
    denominator = denominator + continuing[:, None] * jnp.einsum(
        "ihd,hd->ih", query_wide, total_in, precision=EXACT_MODE
    )
    context = numerator / denominator[:, :, None]
    context_low = lax.dynamic_slice_in_dim(context.reshape(span, width), own_start, rows).astype(
        jnp.bfloat16
    )
    attended = jnp.dot(context_low, out_weight, preferred_element_type=jnp.float32)
    residual = inputs + attended
    normed_two, scaled_two, inv_two = normalize(residual, norm2_gain, norm2_shift)
    second_low = normed_two.astype(jnp.bfloat16)
    cotangent_wide = cotangent.astype(jnp.float32)
    group_second = lax.all_gather(second_low, "mp", axis=0, tiled=True)
    hidden_in = jnp.dot(group_second, up_weight, preferred_element_type=jnp.float32) + up_bias
    hidden_low = jax.nn.gelu(hidden_in, approximate=False).astype(jnp.bfloat16)
    ffn_out = lax.psum_scatter(
        jnp.dot(hidden_low, down_weight, preferred_element_type=jnp.float32).astype(jnp.bfloat16),
        "mp",
        scatter_dimension=0,
        tiled=True,
    ).astype(jnp.float32)
    group_cotangent = lax.all_gather(cotangent, "mp", axis=0, tiled=True)
    grad_down = jnp.einsum(
        "tf,td->fd", hidden_low, group_cotangent, preferred_element_type=jnp.float32
    )
    grad_hidden = jnp.einsum(
        "td,fd->tf", group_cotangent, down_weight, preferred_element_type=jnp.float32
    )
    hidden_grad = (grad_hidden * gelu_slope(hidden_in)).astype(jnp.bfloat16)
    grad_up_bias = jnp.sum(hidden_grad.astype(jnp.float32), axis=0)
    grad_up = jnp.einsum("td,tf->df", group_second, hidden_grad, preferred_element_type=jnp.float32)
    grad_second = lax.psum_scatter(
        jnp.einsum("tf,df->td", hidden_grad, up_weight, preferred_element_type=jnp.float32).astype(
            jnp.bfloat16
        ),
        "mp",
        scatter_dimension=0,
        tiled=True,
    ).astype(jnp.float32)
    grad_up, grad_up_bias, grad_down = lax.psum((grad_up, grad_up_bias, grad_down), "dp")
    output = (residual + ffn_out + down_bias).astype(jnp.bfloat16)
    grad_second_in, grad_gain_two, grad_shift_two = normalize_back(
        grad_second, scaled_two, inv_two, norm2_gain
    )
    grad_residual = cotangent_wide + grad_second_in
    grad_attended = grad_residual.astype(jnp.bfloat16)
    grad_out = jnp.einsum(
        "ti,to->io", context_low, grad_attended, preferred_element_type=jnp.float32
    )
    grad_context_own = jnp.einsum(
        "to,io->ti", grad_attended, out_weight, preferred_element_type=jnp.float32
    ).astype(jnp.bfloat16)
    grad_context = (
        lax.all_gather(grad_context_own, "mp", axis=0, tiled=True)
        .astype(jnp.float32)
        .reshape(span, HEADS, HEAD_DIM)
    )
    grad_numer = (grad_context / denominator[:, :, None]).astype(jnp.bfloat16)
    grad_denom = -jnp.sum(grad_context * context, axis=-1) / denominator
    local_state = jnp.einsum(
        "ihd,ihe->hde",
        query_all * continuing.astype(jnp.bfloat16)[:, None, None],
        grad_numer,
        preferred_element_type=jnp.float32,
    )
    local_total = jnp.einsum(
        "ih,ihd->hd", continuing[:, None] * grad_denom, query_wide, precision=EXACT_MODE
    )
    state_back, total_back, _ = carried_in_2(
        (local_state, local_total, reset), "dp", join_states, (zero_state, zero_total, nothing)
    )
    prior = jnp.concatenate([jnp.ones((1,), jnp.float32), continuing[BLK - 1 :: BLK][:-1]])
    true_states = block_states + prior[:, None, None, None] * state_in[None]
    true_totals = block_totals + prior[:, None, None] * total_in[None]

    def back_block(carry, index):
        state_grad, total_grad = carry
        start = index * BLK
        query, keys, values = features(start)
        query_low = feature_map(query).astype(jnp.bfloat16)
        key_low = feature_map(keys).astype(jnp.bfloat16)
        value_low = values.astype(jnp.bfloat16)
        carried, ending, allowed = block_masks(segment, opening, start)
        state = true_states[index]
        total = true_totals[index]
        numer_grad = lax.dynamic_slice_in_dim(grad_numer, start, BLK)
        denom_grad = lax.dynamic_slice_in_dim(grad_denom, start, BLK)
        scores = (
            jnp.einsum("ihd,jhd->hij", query_low, key_low, preferred_element_type=jnp.float32)
            * allowed[None]
        )
        weights = scores.astype(jnp.bfloat16)
        weight_grad = (
            jnp.einsum("ihe,jhe->hij", numer_grad, value_low, preferred_element_type=jnp.float32)
            + denom_grad.T[:, :, None]
        )
        score_grad = weight_grad.astype(jnp.bfloat16) * allowed.astype(jnp.bfloat16)[None]
        query_wide_blk = query_low.astype(jnp.float32)
        numer_wide = numer_grad.astype(jnp.float32)
        query_grad = jnp.einsum(
            "hij,jhd->ihd", score_grad, key_low, preferred_element_type=jnp.float32
        )
        query_grad = query_grad + carried[:, None, None] * (
            jnp.einsum("ihe,hde->ihd", numer_wide, state, precision=EXACT_MODE)
            + denom_grad[:, :, None] * total[None]
        )
        key_grad = jnp.einsum(
            "hij,ihd->jhd", score_grad, query_low, preferred_element_type=jnp.float32
        )
        key_grad = key_grad + ending[:, None, None] * (
            jnp.einsum(
                "jhe,hde->jhd", value_low.astype(jnp.float32), state_grad, precision=EXACT_MODE
            )
            + total_grad[None]
        )
        value_grad = jnp.einsum(
            "hij,ihd->jhd", weights, numer_grad, preferred_element_type=jnp.float32
        )
        value_grad = value_grad + ending[:, None, None] * jnp.einsum(
            "jhd,hde->jhe", key_low.astype(jnp.float32), state_grad, precision=EXACT_MODE
        )
        keep = carried[-1]
        prev_state = keep * state_grad + jnp.einsum(
            "ihd,ihe->hde",
            query_low * carried.astype(jnp.bfloat16)[:, None, None],
            numer_grad,
            preferred_element_type=jnp.float32,
        )
        prev_total = keep * total_grad + jnp.einsum(
            "ih,ihd->hd", carried[:, None] * denom_grad, query_wide_blk, precision=EXACT_MODE
        )
        joined = jnp.concatenate(
            [
                (query_grad * feature_slope(query)).reshape(BLK, width),
                (key_grad * feature_slope(keys)).reshape(BLK, width),
                value_grad.reshape(BLK, width),
            ],
            axis=1,
        )
        return ((prev_state, prev_total), joined.astype(jnp.bfloat16))

    _, grad_blocks = lax.scan(
        back_block, (state_back, total_back), jnp.arange(blocks, dtype=jnp.int32), reverse=True
    )
    grad_projected = lax.dynamic_slice_in_dim(grad_blocks.reshape(span, 3 * width), own_start, rows)
    grad_qkv = jnp.einsum(
        "td,tk->dk", normed_low, grad_projected, preferred_element_type=jnp.float32
    )
    grad_first = jnp.einsum(
        "tk,dk->td", grad_projected, qkv_weight, preferred_element_type=jnp.float32
    )
    grad_first_in, grad_gain_one, grad_shift_one = normalize_back(
        grad_first, scaled_one, inv_one, norm1_gain
    )
    input_grad = (grad_residual + grad_first_in).astype(jnp.bfloat16)
    grad_down_bias = jnp.sum(cotangent_wide, axis=0)
    summed = lax.psum(
        (
            grad_qkv,
            grad_out,
            grad_gain_one,
            grad_shift_one,
            grad_gain_two,
            grad_shift_two,
            grad_down_bias,
        ),
        ("dp", "mp"),
    )
    return (
        output,
        input_grad,
        summed[0],
        summed[1],
        summed[2],
        summed[3],
        summed[4],
        summed[5],
        grad_up,
        grad_up_bias,
        grad_down,
        summed[6],
    )


def solution(mesh):
    in_specs = (
        P(("dp", "mp"), None),
        P(),
        P(),
        P(),
        P(),
        P(),
        P(),
        P(None, "mp"),
        P("mp"),
        P("mp", None),
        P(),
        P(),
        P(("dp", "mp"), None),
    )
    out_specs = (
        P(("dp", "mp"), None),
        P(("dp", "mp"), None),
        P(),
        P(),
        P(),
        P(),
        P(),
        P(),
        P(None, "mp"),
        P("mp"),
        P("mp", None),
        P(),
    )
    return jax.shard_map(local, mesh=mesh, in_specs=in_specs, out_specs=out_specs, check_vma=False)
```

profile of v0, /device:TPU:0, one launch (start us, length us, event | category | flops | bytes accessed | tf_op | source)
XLA Modules:
  0.0 1671.2 jit_solution(14207868749321259398)
XLA Ops:
  17.8 15.2 all-reduce
  33.1 62.3 %all-gather.9.cloned.1.call-done = bf16[4096,512]{0,1:T(8,128)(2,1)} async-done(((bf16[1024,512]{0,1:T(8,128)(2,1)}), bf16[4096,512]{0,1:T(8,128)(2,1)}) %all-gather.9.cloned.1.call-update) | async-done | bytes 4194320 | tf_op jit(solution)/shard_map/all_gather | solution.py:148
  101.9 482.7 %while.75 = (s32[]{:T(128)}, f32[8,64,64]{2,1,0:T(8,128)S(1)}, f32[8,64]{1,0:T(8,128)S(1)}, f32[8,512,8,64]{1,0,3,2:T(8,128)}, f32[8,512,8]{1,2,0:T(8,128)}, /*i...) while((s32[]{:T(128)}, f32[8,64,64]{2,1,0:T(8,128)S(1)}, ...), condition=%wide.region_8.9_spmd.clone, body=%wide.region_5.8_spmd.clone.sunk | while | flops 1599254528 | bytes 64349520 | solution.py:196
  133.0 21.8 %dynamic_update_slice.51 = f32[8,512,8,64]{1,0,3,2:T(8,128)} dynamic-update-slice(f32[8,512,8,64]{1,0,3,2:T(8,128)} %get-tuple-element.1293, f32[1,512,8,64]{1,0,3,2:T(1,128)S(1)} %copy.224, s32[]{:T(128)} %get-tuple-element.1290, s32[]{:T(128)} %constant.253.clone.1..sunk.2, s32[]{:T(128)} %constant.253.clone.1..sunk.2, s32[]{:T(128)} %constant.253.clone.1..sunk.2) | dynamic-update-slice | bytes 2097156 | tf_op jit(solution)/shard_map/while/body/jit(dynamic_update_index_in_dim)/dynamic_update_slice | solution.py:196
  193.4 21.8 %dynamic_update_slice.51 = f32[8,512,8,64]{1,0,3,2:T(8,128)} dynamic-update-slice(f32[8,512,8,64]{1,0,3,2:T(8,128)} %get-tuple-element.1293, f32[1,512,8,64]{1,0,3,2:T(1,128)S(1)} %copy.224, s32[]{:T(128)} %get-tuple-element.1290, s32[]{:T(128)} %constant.253.clone.1..sunk.2, s32[]{:T(128)} %constant.253.clone.1..sunk.2, s32[]{:T(128)} %constant.253.clone.1..sunk.2) | dynamic-update-slice | bytes 2097156 | tf_op jit(solution)/shard_map/while/body/jit(dynamic_update_index_in_dim)/dynamic_update_slice | solution.py:196
  253.7 21.8 %dynamic_update_slice.51 = f32[8,512,8,64]{1,0,3,2:T(8,128)} dynamic-update-slice(f32[8,512,8,64]{1,0,3,2:T(8,128)} %get-tuple-element.1293, f32[1,512,8,64]{1,0,3,2:T(1,128)S(1)} %copy.224, s32[]{:T(128)} %get-tuple-element.1290, s32[]{:T(128)} %constant.253.clone.1..sunk.2, s32[]{:T(128)} %constant.253.clone.1..sunk.2, s32[]{:T(128)} %constant.253.clone.1..sunk.2) | dynamic-update-slice | bytes 2097156 | tf_op jit(solution)/shard_map/while/body/jit(dynamic_update_index_in_dim)/dynamic_update_slice | solution.py:196
  314.0 21.8 %dynamic_update_slice.51 = f32[8,512,8,64]{1,0,3,2:T(8,128)} dynamic-update-slice(f32[8,512,8,64]{1,0,3,2:T(8,128)} %get-tuple-element.1293, f32[1,512,8,64]{1,0,3,2:T(1,128)S(1)} %copy.224, s32[]{:T(128)} %get-tuple-element.1290, s32[]{:T(128)} %constant.253.clone.1..sunk.2, s32[]{:T(128)} %constant.253.clone.1..sunk.2, s32[]{:T(128)} %constant.253.clone.1..sunk.2) | dynamic-update-slice | bytes 2097156 | tf_op jit(solution)/shard_map/while/body/jit(dynamic_update_index_in_dim)/dynamic_update_slice | solution.py:196
  374.4 21.8 %dynamic_update_slice.51 = f32[8,512,8,64]{1,0,3,2:T(8,128)} dynamic-update-slice(f32[8,512,8,64]{1,0,3,2:T(8,128)} %get-tuple-element.1293, f32[1,512,8,64]{1,0,3,2:T(1,128)S(1)} %copy.224, s32[]{:T(128)} %get-tuple-element.1290, s32[]{:T(128)} %constant.253.clone.1..sunk.2, s32[]{:T(128)} %constant.253.clone.1..sunk.2, s32[]{:T(128)} %constant.253.clone.1..sunk.2) | dynamic-update-slice | bytes 2097156 | tf_op jit(solution)/shard_map/while/body/jit(dynamic_update_index_in_dim)/dynamic_update_slice | solution.py:196
  434.7 21.8 %dynamic_update_slice.51 = f32[8,512,8,64]{1,0,3,2:T(8,128)} dynamic-update-slice(f32[8,512,8,64]{1,0,3,2:T(8,128)} %get-tuple-element.1293, f32[1,512,8,64]{1,0,3,2:T(1,128)S(1)} %copy.224, s32[]{:T(128)} %get-tuple-element.1290, s32[]{:T(128)} %constant.253.clone.1..sunk.2, s32[]{:T(128)} %constant.253.clone.1..sunk.2, s32[]{:T(128)} %constant.253.clone.1..sunk.2) | dynamic-update-slice | bytes 2097156 | tf_op jit(solution)/shard_map/while/body/jit(dynamic_update_index_in_dim)/dynamic_update_slice | solution.py:196
  495.0 21.8 %dynamic_update_slice.51 = f32[8,512,8,64]{1,0,3,2:T(8,128)} dynamic-update-slice(f32[8,512,8,64]{1,0,3,2:T(8,128)} %get-tuple-element.1293, f32[1,512,8,64]{1,0,3,2:T(1,128)S(1)} %copy.224, s32[]{:T(128)} %get-tuple-element.1290, s32[]{:T(128)} %constant.253.clone.1..sunk.2, s32[]{:T(128)} %constant.253.clone.1..sunk.2, s32[]{:T(128)} %constant.253.clone.1..sunk.2) | dynamic-update-slice | bytes 2097156 | tf_op jit(solution)/shard_map/while/body/jit(dynamic_update_index_in_dim)/dynamic_update_slice | solution.py:196
  555.3 21.8 %dynamic_update_slice.51 = f32[8,512,8,64]{1,0,3,2:T(8,128)} dynamic-update-slice(f32[8,512,8,64]{1,0,3,2:T(8,128)} %get-tuple-element.1293, f32[1,512,8,64]{1,0,3,2:T(1,128)S(1)} %copy.224, s32[]{:T(128)} %get-tuple-element.1290, s32[]{:T(128)} %constant.253.clone.1..sunk.2, s32[]{:T(128)} %constant.253.clone.1..sunk.2, s32[]{:T(128)} %constant.253.clone.1..sunk.2) | dynamic-update-slice | bytes 2097156 | tf_op jit(solution)/shard_map/while/body/jit(dynamic_update_index_in_dim)/dynamic_update_slice | solution.py:196
  584.6 10.9 all-gather
  604.6 22.9 %while.76 = (s32[]{:T(128)}, f32[8,64,64]{2,1,0:T(8,128)}, f32[8,64]{1,0:T(8,128)S(1)}, s32[]{:T(128)}, bf16[8,8,64,64]{3,2,1,0:T(8,128)(2,1)S(1)}, /*index=5*/b...) while((s32[]{:T(128)}, f32[8,64,64]{2,1,0:T(8,128)}, ...), condition=%wide.region_10.11_spmd.clone, body=%wide.region_9.10_spmd.clone.sunk | while | flops 166405 | bytes 332957 | solution.py:34
  660.8 76.4 %all-gather.11.cloned.1.call-done = bf16[4096,512]{0,1:T(8,128)(2,1)} async-done(((bf16[1024,512]{0,1:T(8,128)(2,1)}), bf16[4096,512]{0,1:T(8,128)(2,1)}) %all-gather.11.cloned.1.call-update) | async-done | bytes 4194320 | tf_op jit(solution)/shard_map/all_gather | solution.py:223
  737.2 22.8 %fusion.89 = (bf16[4096,512]{1,0:T(8,128)(2,1)}, f32[4096,512]{1,0:T(8,128)}) fusion(f32[512]{0:T(512)} %convert_element_type.335, bf16[4096,512]{0,1:T(8,128)(2,1)} %all-gather.11.cloned.1.call-done, bf16[512,512]{1,0:T(8,128)(2,1)S(1)} %copy-done), kind=kOutput, calls=%fused_computation.135 | convolution fusion | flops 2285895680 | bytes 17303552 | tf_op jit(solution)/shard_map/dot_general | solution.py:224
  760.0 58.0 %all-gather.13.cloned.1.call-done = bf16[4096,512]{1,0:T(8,128)(2,1)} async-done(((bf16[1024,512]{1,0:T(8,128)(2,1)}), bf16[4096,512]{1,0:T(8,128)(2,1)}) %all-gather.13.cloned.1.call-update) | async-done | bytes 4194320 | tf_op jit(solution)/shard_map/all_gather | solution.py:232
  853.7 55.1 %reduce-scatter.5.cloned.1.call-done = bf16[1024,512]{0,1:T(8,128)(2,1)} async-done(((bf16[4096,512]{0,1:T(8,128)(2,1)}), bf16[1024,512]{0,1:T(8,128)(2,1)}) %reduce-scatter.5.cloned.1.call-update) | async-done | bytes 1048592 | tf_op jit(solution)/shard_map/reduce_scatter | solution.py:242
  911.5 76.8 %reduce-scatter.3.cloned.1.call-done = bf16[1024,512]{0,1:T(8,128)(2,1)} async-done(((bf16[4096,512]{0,1:T(8,128)(2,1)}), bf16[1024,512]{0,1:T(8,128)(2,1)}) %reduce-scatter.3.cloned.1.call-update) | async-done | bytes 1048592 | tf_op jit(solution)/shard_map/reduce_scatter | solution.py:226
  1011.1 66.3 %all-gather.15.cloned.1.call-done = bf16[4096,512]{1,0:T(8,128)(2,1)} async-done(((bf16[1024,512]{1,0:T(8,128)(2,1)}), bf16[4096,512]{1,0:T(8,128)(2,1)}) %all-gather.15.cloned.1.call-update) | async-done | bytes 4194320 | tf_op jit(solution)/shard_map/all_gather | solution.py:264
  1111.1 13.4 all-gather.2
  1139.8 371.0 %while.74 = (s32[]{:T(128)}, f32[8,64,64]{2,1,0:T(8,128)S(1)}, f32[8,64]{1,0:T(8,128)S(1)}, bf16[8,512,1536]{2,1,0:T(8,128)(2,1)}, s32[8]{0:T(128)S(1)}, /*index...) while((s32[]{:T(128)}, f32[8,64,64]{2,1,0:T(8,128)S(1)}, ...), condition=%wide.region_21.22_spmd, body=%wide.region_20.21_spmd.sunk | while | flops 2815500288 | bytes 89005016 | solution.py:352
  1517.2 12.9 psum.77
  1546.3 38.9 %all-reduce.1 = (f32[512]{0:T(512)}, f32[512]{0:T(512)}, f32[512]{0:T(512)}, f32[512]{0:T(512)}, f32[512]{0:T(512)}) all-reduce(f32[512]{0:T(512)S(1)} %get-tuple-element.848, f32[512]{0:T(512)S(1)} %get-tuple-element.977, f32[512]{0:T(512)S(1)} %copy-done.48, f32[512]{0:T(512)S(1)} %copy-done.49, ...), channel_id=1, replica_groups=mesh['dp'=8,'mp'=4] {'dp','mp'}, use_global_device_ids=true, to_apply=%region_27.28 | all-reduce | flops 2560 | bytes 20480 | tf_op jit(solution)/shard_map/psum | solution.py:367
  1585.2 71.9 %all-reduce.7.cloned.1.call-done = (f32[512,1536]{1,0:T(8,128)}, f32[512,512]{1,0:T(8,128)}) async-done(((f32[512,1536]{1,0:T(8,128)}, f32[512,512]{1,0:T(8,128)}), (f32[512,1536]{1,0:T(8,128)}, f32[512,512]{1,0:T(8,128)})) %all-reduce.7.cloned.1.call-update) | async-done | bytes 4194320 | tf_op jit(solution)/shard_map/psum | solution.py:367
  (765 shorter events, 861.3 us)
Async XLA Ops:
  7.2 730.0 %copy-start = (bf16[512,512]{1,0:T(8,128)(2,1)S(1)}, bf16[512,512]{1,0:T(8,128)(2,1)}, u32[]{:S(2)}) copy-start(bf16[512,512]{1,0:T(8,128)(2,1)} %param.28) | copy-start | bytes 1572868
  7.2 8.6 copy-start.59
  7.2 88.1 %all-gather.9.cloned.1.call-start = ((), (), s32[]{:S(2)}) async-start(), calls=%async_computation.2 | async-start | bytes 5242880 | tf_op jit(solution)/shard_map/all_gather | solution.py:148
  8.8 93.1 %copy-start.7 = (bf16[1024,512]{0,1:T(8,128)(2,1)}, bf16[1024,512]{0,1:T(8,128)(2,1)S(1)}, u32[]{:S(2)}) copy-start(bf16[1024,512]{0,1:T(8,128)(2,1)S(1)} %copy.149) | copy-start | bytes 3145732
  11.8 725.5 %all-gather.11.cloned.1.call-start = ((), (), s32[]{:S(2)}) async-start(), calls=%async_computation.3 | async-start | bytes 5242880 | tf_op jit(solution)/shard_map/all_gather | solution.py:223
  15.2 86.6 %copy-start.28 = (f32[4096]{0:T(1024)}, f32[4096]{0:T(1024)S(1)}, u32[]{:S(2)}) copy-start(f32[4096]{0:T(1024)S(1)} %get-tuple-element.953) | copy-start | bytes 49156
  584.6 11.0 copy-start.45
  627.6 14.3 copy-start.26
  632.4 13.5 copy-start.29
  632.4 13.5 copy-start.31
  646.0 7.0 copy-start.8
  658.8 159.3 %all-gather.13.cloned.1.call-start = ((), (), s32[]{:S(2)}) async-start(), calls=%async_computation.5 | async-start | bytes 5242880 | tf_op jit(solution)/shard_map/all_gather | solution.py:232
  659.5 249.3 %reduce-scatter.5.cloned.1.call-start = ((), (), s32[]{:S(2)}) async-start(), calls=%async_computation.6 | async-start | bytes 5242880 | tf_op jit(solution)/shard_map/reduce_scatter | solution.py:242
  833.3 154.9 %reduce-scatter.3.cloned.1.call-start = ((), (), s32[]{:S(2)}) async-start(), calls=%async_computation.4 | async-start | bytes 5242880 | tf_op jit(solution)/shard_map/reduce_scatter | solution.py:226
  840.9 67.9 %copy-start.33 = (f32[1024]{0:T(1024)S(1)}, f32[1024]{0:T(1024)}, u32[]{:S(2)}) copy-start(f32[1024]{0:T(1024)} %copy-done.32) | copy-start | bytes 12292
  840.9 67.9 %copy-start.37 = (f32[1024]{0:T(1024)S(1)}, f32[1024]{0:T(1024)}, u32[]{:S(2)}) copy-start(f32[1024]{0:T(1024)} %copy-done.36) | copy-start | bytes 12292
  840.9 67.9 %copy-start.42 = (f32[512]{0:T(512)S(1)}, f32[512]{0:T(512)}, u32[]{:S(2)}) copy-start(f32[512]{0:T(512)} %param.26) | copy-start | bytes 6148
  840.9 147.3 %copy-start.51 = (f32[512]{0:T(512)S(1)}, f32[512]{0:T(512)}, u32[]{:S(2)}) copy-start(f32[512]{0:T(512)} %param.31) | copy-start | bytes 6148
  840.9 236.4 %all-gather.15.cloned.1.call-start = ((), (), s32[]{:S(2)}) async-start(), calls=%async_computation.7 | async-start | bytes 5242880 | tf_op jit(solution)/shard_map/all_gather | solution.py:264
  996.0 589.2 %all-reduce.9.cloned.1.call-start = ((), (), s32[]{:S(2)}) async-start(), calls=%async_computation.9 | async-start | bytes 4194304 | tf_op jit(solution)/shard_map/psum | solution.py:250
  1007.7 649.3 %all-reduce.7.cloned.1.call-start = ((), (), s32[]{:S(2)}) async-start(), calls=%async_computation.8 | async-start | bytes 8388608 | tf_op jit(solution)/shard_map/psum | solution.py:367
  1084.4 22.6 %copy-start.5 = (f32[4096,512]{0,1:T(8,128)S(1)}, f32[4096,512]{0,1:T(8,128)}, u32[]{:S(2)}) copy-start(f32[4096,512]{0,1:T(8,128)} %copy.158) | copy-start | bytes 25165828
  1109.8 14.7 copy-start.58
  1516.5 13.6 copy-start.20
  (73 other events, 242.4 us)
Sparse Core Ops, SparseCore 0:
  11.9 83.4 all-gather.8
  658.9 78.2 all-gather.10
  738.8 79.2 all-gather.12
  833.4 75.2 reduce-scatter.4
  910.9 77.2 reduce-scatter.2
  996.1 81.2 all-gather.14
  1080.7 61.3 all-reduce.8
  1516.7 140.3 all-reduce.6
where the time goes:
time: 1690 us; the launch traced here: 1670 us
  waiting for transfers between devices  468 us (28%)
  local copies, waits for them, and re-layouts  449 us (27%)
  matrix products  431 us (26%)
  other arithmetic  139 us (8%)
  blocking collectives  109 us (6%)
  loops' own time  48.6 us (3%)
    dynamic_update_slice x16, local copies, waits for them, and re-layouts, local(): lax.scan(forward_block, (zero_state, zero_total), jnp.arange(blocks, dtyp...  183 us
    reduce_scatter x1, waiting for transfers between devices, local(): lax.psum_scatter(jnp.dot(hidden_low, down_weight, preferred_element_type=...  76.8 us
    all_gather x1, waiting for transfers between devices, local(): group_second = lax.all_gather(second_low, 'mp', axis=0, tiled=True)  76.4 us
    psum x1, waiting for transfers between devices, local(): lax.psum((grad_qkv, grad_out, grad_gain_one, grad_shift_one, grad_gain_tw...  71.9 us
    all_gather x1, waiting for transfers between devices, local(): lax.all_gather(grad_context_own, 'mp', axis=0, tiled=True)  66.3 us
    all_gather x1, waiting for transfers between devices, local(): group_rows = lax.all_gather(normed_low, 'mp', axis=0, tiled=True)  62.3 us
    all_gather x1, waiting for transfers between devices, local(): group_cotangent = lax.all_gather(cotangent, 'mp', axis=0, tiled=True)  58 us
    reduce_scatter x1, waiting for transfers between devices, local(): lax.psum_scatter(jnp.einsum('tf,df->td', hidden_grad, up_weight, preferre...  55.1 us
  transfers between devices with their start and end apart: 8, of which 7 were waited for; matrix products, arithmetic and copies ran while one was open for 26% of the time, Pallas kernels for 0%

commit v1 on v0

--- a/solution.py
+++ b/solution.py
@@ -220,7 +220,15 @@
     normed_two, scaled_two, inv_two = normalize(residual, norm2_gain, norm2_shift)
     second_low = normed_two.astype(jnp.bfloat16)
     cotangent_wide = cotangent.astype(jnp.float32)
-    group_second = lax.all_gather(second_low, "mp", axis=0, tiled=True)
+    ways, here = (lax.axis_size("mp"), lax.axis_index("mp"))
+    grown, reach = (second_low, 1)
+    while reach < ways:
+        theirs = lax.ppermute(grown, "mp", [(d, d ^ reach) for d in range(ways)])
+        mine_first = jnp.concatenate([grown, theirs], axis=0)
+        theirs_first = jnp.concatenate([theirs, grown], axis=0)
+        grown = jnp.where(here & reach == 0, mine_first, theirs_first)
+        reach = 2 * reach
+    group_second = grown
     hidden_in = jnp.dot(group_second, up_weight, preferred_element_type=jnp.float32) + up_bias
     hidden_low = jax.nn.gelu(hidden_in, approximate=False).astype(jnp.bfloat16)
     ffn_out = lax.psum_scatter(

time: 1690 us -> 1750 us (1.036)
  waiting for transfers between devices: 468 us -> 529 us
    ppermute x0 -> x2, waiting for transfers between devices: none -> 184 us  [local(): theirs = lax.ppermute(grown, 'mp', [(d, d ^ reach) for d in range(ways)])]
    all_gather x1 -> x0, waiting for transfers between devices: 76.4 us -> none  [local(): group_second = lax.all_gather(second_low, 'mp', axis=0, tiled=True)]
    all_gather x1, waiting for transfers between devices: 58 us -> 0.01 us  [local(): group_cotangent = lax.all_gather(cotangent, 'mp', axis=0, tiled=True)]
  transfers between devices with their start and end apart: 8 -> 9, of which waited for: 7 -> 7; matrix products, arithmetic and copies ran while one was open for 26% -> 26% of each run, Pallas kernels for 0% -> 0%
where the time goes in v1:
time: 1750 us; the launch traced here: 1730 us
  waiting for transfers between devices  529 us (30%)
  matrix products  438 us (25%)
  local copies, waits for them, and re-layouts  436 us (25%)
  other arithmetic  151 us (9%)
  blocking collectives  110 us (6%)
  loops' own time  48.8 us (3%)
    ppermute x2, waiting for transfers between devices, local(): theirs = lax.ppermute(grown, 'mp', [(d, d ^ reach) for d in range(ways)])  184 us
    dynamic_update_slice x16, local copies, waits for them, and re-layouts, local(): lax.scan(forward_block, (zero_state, zero_total), jnp.arange(blocks, dtyp...  184 us
    psum x1, waiting for transfers between devices, local(): lax.psum((grad_qkv, grad_out, grad_gain_one, grad_shift_one, grad_gain_tw...  78.5 us
    reduce_scatter x1, waiting for transfers between devices, local(): lax.psum_scatter(jnp.dot(hidden_low, down_weight, preferred_element_type=...  76.5 us
    reduce_scatter x1, waiting for transfers between devices, local(): lax.psum_scatter(jnp.einsum('tf,df->td', hidden_grad, up_weight, preferre...  66.5 us
    all_gather x1, waiting for transfers between devices, local(): lax.all_gather(grad_context_own, 'mp', axis=0, tiled=True)  62.1 us
    all_gather x1, waiting for transfers between devices, local(): group_rows = lax.all_gather(normed_low, 'mp', axis=0, tiled=True)  61.3 us
    dot_general x8, matrix products, forward_block(): jnp.einsum('ihd,jhd->hij', query_low, key_low, preferred_element_type=jnp...  46.3 us
  transfers between devices with their start and end apart: 9, of which 7 were waited for; matrix products, arithmetic and copies ran while one was open for 26% of the time, Pallas kernels for 0%

profile of v1, /device:TPU:0, one launch (start us, length us, event | category | flops | bytes accessed | tf_op | source)
XLA Modules:
  0.0 1731.1 jit_solution(11487449149077086337)
XLA Ops:
  20.4 15.5 all-reduce
  36.0 61.3 %all-gather.8.cloned.1.call-done = bf16[4096,512]{1,0:T(8,128)(2,1)} async-done(((bf16[1024,512]{1,0:T(8,128)(2,1)}), bf16[4096,512]{1,0:T(8,128)(2,1)}) %all-gather.8.cloned.1.call-update) | async-done | bytes 4194320 | tf_op jit(solution)/shard_map/all_gather | solution.py:148
  97.4 483.3 %while.75 = (s32[]{:T(128)}, f32[8,64,64]{2,1,0:T(8,128)S(1)}, f32[8,64]{1,0:T(8,128)S(1)}, f32[8,512,8,64]{1,0,3,2:T(8,128)}, f32[8,512,8]{1,2,0:T(8,128)}, /*i...) while((s32[]{:T(128)}, f32[8,64,64]{2,1,0:T(8,128)S(1)}, ...), condition=%wide.region_8.9_spmd.clone, body=%wide.region_5.8_spmd.clone.sunk | while | flops 1599254528 | bytes 64349520 | solution.py:196
  128.5 21.9 %dynamic_update_slice.51 = f32[8,512,8,64]{1,0,3,2:T(8,128)} dynamic-update-slice(f32[8,512,8,64]{1,0,3,2:T(8,128)} %get-tuple-element.1103, f32[1,512,8,64]{1,0,3,2:T(1,128)S(1)} %copy.172, s32[]{:T(128)} %get-tuple-element.1100, s32[]{:T(128)} %constant.255.clone.1..sunk.2, s32[]{:T(128)} %constant.255.clone.1..sunk.2, s32[]{:T(128)} %constant.255.clone.1..sunk.2) | dynamic-update-slice | bytes 2097156 | tf_op jit(solution)/shard_map/while/body/jit(dynamic_update_index_in_dim)/dynamic_update_slice | solution.py:196
  189.0 21.9 %dynamic_update_slice.51 = f32[8,512,8,64]{1,0,3,2:T(8,128)} dynamic-update-slice(f32[8,512,8,64]{1,0,3,2:T(8,128)} %get-tuple-element.1103, f32[1,512,8,64]{1,0,3,2:T(1,128)S(1)} %copy.172, s32[]{:T(128)} %get-tuple-element.1100, s32[]{:T(128)} %constant.255.clone.1..sunk.2, s32[]{:T(128)} %constant.255.clone.1..sunk.2, s32[]{:T(128)} %constant.255.clone.1..sunk.2) | dynamic-update-slice | bytes 2097156 | tf_op jit(solution)/shard_map/while/body/jit(dynamic_update_index_in_dim)/dynamic_update_slice | solution.py:196
  249.4 21.9 %dynamic_update_slice.51 = f32[8,512,8,64]{1,0,3,2:T(8,128)} dynamic-update-slice(f32[8,512,8,64]{1,0,3,2:T(8,128)} %get-tuple-element.1103, f32[1,512,8,64]{1,0,3,2:T(1,128)S(1)} %copy.172, s32[]{:T(128)} %get-tuple-element.1100, s32[]{:T(128)} %constant.255.clone.1..sunk.2, s32[]{:T(128)} %constant.255.clone.1..sunk.2, s32[]{:T(128)} %constant.255.clone.1..sunk.2) | dynamic-update-slice | bytes 2097156 | tf_op jit(solution)/shard_map/while/body/jit(dynamic_update_index_in_dim)/dynamic_update_slice | solution.py:196
  309.8 21.9 %dynamic_update_slice.51 = f32[8,512,8,64]{1,0,3,2:T(8,128)} dynamic-update-slice(f32[8,512,8,64]{1,0,3,2:T(8,128)} %get-tuple-element.1103, f32[1,512,8,64]{1,0,3,2:T(1,128)S(1)} %copy.172, s32[]{:T(128)} %get-tuple-element.1100, s32[]{:T(128)} %constant.255.clone.1..sunk.2, s32[]{:T(128)} %constant.255.clone.1..sunk.2, s32[]{:T(128)} %constant.255.clone.1..sunk.2) | dynamic-update-slice | bytes 2097156 | tf_op jit(solution)/shard_map/while/body/jit(dynamic_update_index_in_dim)/dynamic_update_slice | solution.py:196
  370.2 21.9 %dynamic_update_slice.51 = f32[8,512,8,64]{1,0,3,2:T(8,128)} dynamic-update-slice(f32[8,512,8,64]{1,0,3,2:T(8,128)} %get-tuple-element.1103, f32[1,512,8,64]{1,0,3,2:T(1,128)S(1)} %copy.172, s32[]{:T(128)} %get-tuple-element.1100, s32[]{:T(128)} %constant.255.clone.1..sunk.2, s32[]{:T(128)} %constant.255.clone.1..sunk.2, s32[]{:T(128)} %constant.255.clone.1..sunk.2) | dynamic-update-slice | bytes 2097156 | tf_op jit(solution)/shard_map/while/body/jit(dynamic_update_index_in_dim)/dynamic_update_slice | solution.py:196
  430.6 21.9 %dynamic_update_slice.51 = f32[8,512,8,64]{1,0,3,2:T(8,128)} dynamic-update-slice(f32[8,512,8,64]{1,0,3,2:T(8,128)} %get-tuple-element.1103, f32[1,512,8,64]{1,0,3,2:T(1,128)S(1)} %copy.172, s32[]{:T(128)} %get-tuple-element.1100, s32[]{:T(128)} %constant.255.clone.1..sunk.2, s32[]{:T(128)} %constant.255.clone.1..sunk.2, s32[]{:T(128)} %constant.255.clone.1..sunk.2) | dynamic-update-slice | bytes 2097156 | tf_op jit(solution)/shard_map/while/body/jit(dynamic_update_index_in_dim)/dynamic_update_slice | solution.py:196
  491.0 21.9 %dynamic_update_slice.51 = f32[8,512,8,64]{1,0,3,2:T(8,128)} dynamic-update-slice(f32[8,512,8,64]{1,0,3,2:T(8,128)} %get-tuple-element.1103, f32[1,512,8,64]{1,0,3,2:T(1,128)S(1)} %copy.172, s32[]{:T(128)} %get-tuple-element.1100, s32[]{:T(128)} %constant.255.clone.1..sunk.2, s32[]{:T(128)} %constant.255.clone.1..sunk.2, s32[]{:T(128)} %constant.255.clone.1..sunk.2) | dynamic-update-slice | bytes 2097156 | tf_op jit(solution)/shard_map/while/body/jit(dynamic_update_index_in_dim)/dynamic_update_slice | solution.py:196
  551.4 21.9 %dynamic_update_slice.51 = f32[8,512,8,64]{1,0,3,2:T(8,128)} dynamic-update-slice(f32[8,512,8,64]{1,0,3,2:T(8,128)} %get-tuple-element.1103, f32[1,512,8,64]{1,0,3,2:T(1,128)S(1)} %copy.172, s32[]{:T(128)} %get-tuple-element.1100, s32[]{:T(128)} %constant.255.clone.1..sunk.2, s32[]{:T(128)} %constant.255.clone.1..sunk.2, s32[]{:T(128)} %constant.255.clone.1..sunk.2) | dynamic-update-slice | bytes 2097156 | tf_op jit(solution)/shard_map/while/body/jit(dynamic_update_index_in_dim)/dynamic_update_slice | solution.py:196
  580.8 10.9 all-gather
  600.8 22.8 %while.76 = (s32[]{:T(128)}, f32[8,64,64]{2,1,0:T(8,128)}, f32[8,64]{1,0:T(8,128)S(1)}, s32[]{:T(128)}, bf16[8,8,64,64]{3,2,1,0:T(8,128)(2,1)S(1)}, /*index=5*/b...) while((s32[]{:T(128)}, f32[8,64,64]{2,1,0:T(8,128)}, ...), condition=%wide.region_10.11_spmd.clone, body=%wide.region_9.10_spmd.clone.sunk | while | flops 166405 | bytes 332957 | solution.py:34
  652.5 25.7 %collective-permute-done = bf16[1024,512]{1,0:T(8,128)(2,1)} collective-permute-done((bf16[1024,512]{1,0:T(8,128)(2,1)}, bf16[1024,512]{1,0:T(8,128)(2,1)}, u32[]{:S(2)}, u32[]{:S(2)}) %collective-permute-start) | collective-permute-done | bytes 1048608 | tf_op jit(solution)/shard_map/ppermute | solution.py:226
  684.4 158.6 %collective-permute-done.1 = bf16[2048,512]{1,0:T(8,128)(2,1)} collective-permute-done((bf16[2048,512]{1,0:T(8,128)(2,1)}, bf16[2048,512]{1,0:T(8,128)(2,1)}, u32[]{:S(2)}, u32[]{:S(2)}) %collective-permute-start.1) | collective-permute-done | bytes 2097184 | tf_op jit(solution)/shard_map/ppermute | solution.py:226
  843.0 25.0 %fusion.89 = (bf16[4096,512]{1,0:T(8,128)(2,1)}, f32[4096,512]{1,0:T(8,128)}) fusion(f32[512]{0:T(512)S(1)} %convert_element_type.335, bf16[512,512]{1,0:T(8,128)(2,1)S(1)} %copy-done, bf16[2048,512]{1,0:T(8,128)(2,1)} %collective-permute-done.1, bf16[2048,512]{1,0:T(8,128)(2,1)} %maximum_select_fusion.1, pred[]{:T(512)S(6)} %eq.158), kind=kOutput, calls=%fused_computation.135 | convolution fusion | flops 2304770048 | bytes 17303552 | tf_op jit(solution)/shard_map/dot_general | solution.py:232
  891.2 66.5 %reduce-scatter.5.cloned.1.call-done = bf16[1024,512]{1,0:T(8,128)(2,1)} async-done(((bf16[4096,512]{1,0:T(8,128)(2,1)}), bf16[1024,512]{1,0:T(8,128)(2,1)}) %reduce-scatter.5.cloned.1.call-update) | async-done | bytes 1048592 | tf_op jit(solution)/shard_map/reduce_scatter | solution.py:250
  960.6 76.5 %reduce-scatter.3.cloned.1.call-done = bf16[1024,512]{1,0:T(8,128)(2,1)} async-done(((bf16[4096,512]{1,0:T(8,128)(2,1)}), bf16[1024,512]{1,0:T(8,128)(2,1)}) %reduce-scatter.3.cloned.1.call-update) | async-done | bytes 1048592 | tf_op jit(solution)/shard_map/reduce_scatter | solution.py:234
  1063.5 62.1 %all-gather.12.cloned.1.call-done = bf16[4096,512]{1,0:T(8,128)(2,1)} async-done(((bf16[1024,512]{1,0:T(8,128)(2,1)}), bf16[4096,512]{1,0:T(8,128)(2,1)}) %all-gather.12.cloned.1.call-update) | async-done | bytes 4194320 | tf_op jit(solution)/shard_map/all_gather | solution.py:272
  1159.4 13.1 all-gather.2
  1188.1 382.5 %while.74 = (s32[]{:T(128)}, f32[8,64,64]{2,1,0:T(8,128)S(1)}, f32[8,64]{1,0:T(8,128)S(1)}, bf16[8,512,1536]{2,1,0:T(8,128)(2,1)}, s32[8]{0:T(128)S(1)}, /*index...) while((s32[]{:T(128)}, f32[8,64,64]{2,1,0:T(8,128)S(1)}, ...), condition=%wide.region_21.22_spmd, body=%wide.region_20.21_spmd.sunk | while | flops 2815500288 | bytes 89005016 | solution.py:360
  1576.9 12.6 psum.77
  1595.8 39.5 %all-reduce.1 = (f32[512]{0:T(512)}, f32[512]{0:T(512)}, f32[512]{0:T(512)}, f32[512]{0:T(512)}, f32[512]{0:T(512)}) all-reduce(f32[512]{0:T(512)S(1)} %get-tuple-element.658, f32[512]{0:T(512)S(1)} %get-tuple-element.661, f32[512]{0:T(512)S(1)} %copy-done.37, f32[512]{0:T(512)S(1)} %copy-done.38, ...), channel_id=1, replica_groups=mesh['dp'=8,'mp'=4] {'dp','mp'}, use_global_device_ids=true, to_apply=%region_27.28 | all-reduce | flops 2560 | bytes 20480 | tf_op jit(solution)/shard_map/psum | solution.py:375
  1638.5 78.5 %all-reduce.7.cloned.1.call-done = (f32[512,1536]{1,0:T(8,128)}, f32[512,512]{1,0:T(8,128)}) async-done(((f32[512,1536]{1,0:T(8,128)}, f32[512,512]{1,0:T(8,128)}), (f32[512,1536]{1,0:T(8,128)}, f32[512,512]{1,0:T(8,128)})) %all-reduce.7.cloned.1.call-update) | async-done | bytes 4194320 | tf_op jit(solution)/shard_map/psum | solution.py:375
  (738 shorter events, 855.6 us)
Async XLA Ops:
  7.2 835.8 %copy-start = (bf16[512,512]{1,0:T(8,128)(2,1)S(1)}, bf16[512,512]{1,0:T(8,128)(2,1)}, u32[]{:S(2)}) copy-start(bf16[512,512]{1,0:T(8,128)(2,1)} %param.28) | copy-start | bytes 1572868
  7.2 11.2 copy-start.47
  7.2 90.2 %all-gather.8.cloned.1.call-start = ((), (), s32[]{:S(2)}) async-start(), calls=%async_computation.2 | async-start | bytes 5242880 | tf_op jit(solution)/shard_map/all_gather | solution.py:148
  13.8 854.3 %all-gather.10.cloned.1.call-start = ((), (), s32[]{:S(2)}) async-start(), calls=%async_computation.4 | async-start | bytes 5242880 | tf_op jit(solution)/shard_map/all_gather | solution.py:240
  580.7 11.0 copy-start.33
  580.7 47.6 %copy-start.22 = (s32[4096]{0:T(1024)}, s32[4096]{0:T(1024)S(1)}, u32[]{:S(2)}) copy-start(s32[4096]{0:T(1024)S(1)} %get-tuple-element.1315) | copy-start | bytes 49156
  628.4 13.5 copy-start.24
  628.4 13.5 copy-start.26
  652.5 25.7 %collective-permute-start = (bf16[1024,512]{1,0:T(8,128)(2,1)}, bf16[1024,512]{1,0:T(8,128)(2,1)}, u32[]{:S(2)}, u32[]{:S(2)}) collective-permute-start(bf16[1024,512]{1,0:T(8,128)(2,1)} %add_convert_fusion.2), channel_id=1, source_target_pairs={{0,1},{1,0},{2,3},{3,2},{4,5},{5,4},{6,7},{7,6},{8,9},{9,8},{10,11... | collective-permute-start | bytes 3145736 | tf_op jit(solution)/shard_map/ppermute | solution.py:226
  682.4 160.6 %collective-permute-start.1 = (bf16[2048,512]{1,0:T(8,128)(2,1)}, bf16[2048,512]{1,0:T(8,128)(2,1)}, u32[]{:S(2)}, u32[]{:S(2)}) collective-permute-start(bf16[2048,512]{1,0:T(8,128)(2,1)} %maximum_select_fusion.1), channel_id=1, source_target_pairs={{0,2},{1,3},{2,0},{3,1},{4,6},{5,7},{6,4},{7,5},{8,10},{9,11},{10,... | collective-permute-start | bytes 6291464 | tf_op jit(solution)/shard_map/ppermute | solution.py:226
  683.3 274.4 %reduce-scatter.5.cloned.1.call-start = ((), (), s32[]{:S(2)}) async-start(), calls=%async_computation.5 | async-start | bytes 5242880 | tf_op jit(solution)/shard_map/reduce_scatter | solution.py:250
  684.4 158.6 %copy-start.41 = (f32[512]{0:T(512)}, f32[512]{0:T(512)S(1)}, u32[]{:S(2)}) copy-start(f32[512]{0:T(512)S(1)} %convert_element_type.335) | copy-start | bytes 6148
  883.3 153.9 %reduce-scatter.3.cloned.1.call-start = ((), (), s32[]{:S(2)}) async-start(), calls=%async_computation.3 | async-start | bytes 5242880 | tf_op jit(solution)/shard_map/reduce_scatter | solution.py:234
  890.9 146.2 %copy-start.40 = (f32[512]{0:T(512)S(1)}, f32[512]{0:T(512)}, u32[]{:S(2)}) copy-start(f32[512]{0:T(512)} %param.31) | copy-start | bytes 6148
  890.9 234.7 %all-gather.12.cloned.1.call-start = ((), (), s32[]{:S(2)}) async-start(), calls=%async_computation.6 | async-start | bytes 5242880 | tf_op jit(solution)/shard_map/all_gather | solution.py:272
  1044.3 594.2 %all-reduce.9.cloned.1.call-start = ((), (), s32[]{:S(2)}) async-start(), calls=%async_computation.8 | async-start | bytes 4194304 | tf_op jit(solution)/shard_map/psum | solution.py:258
  1052.8 7.5 copy-start.8
  1060.2 656.8 %all-reduce.7.cloned.1.call-start = ((), (), s32[]{:S(2)}) async-start(), calls=%async_computation.7 | async-start | bytes 8388608 | tf_op jit(solution)/shard_map/psum | solution.py:375
  1132.7 22.5 %copy-start.5 = (f32[4096,512]{0,1:T(8,128)S(1)}, f32[4096,512]{0,1:T(8,128)}, u32[]{:S(2)}) copy-start(f32[4096,512]{0,1:T(8,128)} %copy.113) | copy-start | bytes 25165828
  1158.1 14.4 copy-start.46
  1576.2 13.2 copy-start.28
  1576.2 13.2 copy-start.30
  1576.2 13.2 copy-start.36
  1589.5 45.8 %copy-start.9 = (f32[1024,512]{1,0:T(8,128)S(1)}, f32[1024,512]{1,0:T(8,128)}, u32[]{:S(2)}) copy-start(f32[1024,512]{1,0:T(8,128)} %copy-done.7) | copy-start | bytes 6291460
  (63 other events, 219.8 us)
Sparse Core Ops, SparseCore 0:
  13.9 83.4 all-gather.7
  683.4 148.6 all-gather.9
  883.4 74.2 reduce-scatter.4
  959.8 77.2 reduce-scatter.2
  1044.4 81.2 all-gather.11
  1128.8 61.3 all-reduce.8
  1576.4 140.5 all-reduce.6
